TPU v7x, 32 devices: a whole 2x2x4 slice. The times are simulated.
32 devices in a mesh: grp: 8 (over y, x, core), head: 4 (over z).
Axes of the slice: x: 2, y: 2, z: 4, core: 2. Of those that a mesh axis runs over, the one named last changes fastest.
Arguments:
- q_nope: bfloat16 [4, 64, 128, 128], P(None, 'grp', 'head'), may hold values from -6 to 6
- q_rope: bfloat16 [4, 64, 128, 64], P(None, 'grp', 'head'), may hold values from -512 to 512
- w_absorb_k: bfloat16 [128, 128, 512], P('head'), may hold values from -0.5 to 0.5
- w_absorb_v: bfloat16 [128, 512, 128], P('head'), may hold values from -0.25 to 0.25
- latent_cache: bfloat16 [64, 1024, 576], P(('grp', 'head')), may hold values from -4 to 4
- new_latent: bfloat16 [4, 64, 576], P(None, ('grp', 'head')), may hold values from -6 to 6
- lengths: int32 [64], replicated, may hold values from 128 to 1020, as said below
- moves: int32 [4, 1], P('head'), may hold values from 1 to 7
Outputs:
- attended: bfloat16 [4, 64, 128, 128], P(None, 'grp', 'head')
Inputs may be any that keep to these rules, and one draw needn't show every extreme that they name: lengths[r] counts the live rows of latent_cache[r]; its later rows up to 1024 are padding that no query reads.
All inputs are finite; a program needn't handle non-finite values.
Results may differ from a plain program's by a relative error of at most 0.0077.
Values may be sent and summed in bfloat16 or wider, within the bound.
A program may use at most 64 MiB of HBM per device.

v0:
```python
import math
import jax
import jax.numpy as jnp
from jax import lax
from jax.sharding import PartitionSpec as P

HEAD_DIM = 128
ROPE = 64
LATENT = 512
BLOCK = 128
yarn_gain = (0.1 * math.log(40.0) + 1.0) ** 2


def passed_along(value, axis, steps):
    count = lax.axis_size(axis)
    pairs = [(source, (source + steps) % count) for source in range(count)]
    return lax.ppermute(value, axis, pairs)


def attend(queries, stored, counts, recent, moment, window, score_scale):
    holders = queries.shape[0]
    head_count = queries.shape[1]
    capacity = stored.shape[1]
    longest = jnp.max(counts)
    passes = (longest + window - 1) // window
    positions = jnp.arange(window, dtype=jnp.int32)

    def score_tile(tile_index, buffer):
        begin_at = tile_index * window
        key_rows = lax.dynamic_slice_in_dim(stored, begin_at, window, 1)
        partial_value = (
            jnp.einsum("rhc,rtc->rht", queries, key_rows, preferred_element_type=jnp.float32)
            * score_scale
        )
        inside = (begin_at + positions)[None, None, :] < counts[:, None, None]
        partial_value = jnp.where(inside, partial_value, -jnp.inf)
        return lax.dynamic_update_slice_in_dim(buffer, partial_value, begin_at, 2)

    empty = jnp.full((holders, head_count, capacity), -jnp.inf, jnp.float32)
    scores = lax.fori_loop(0, passes, score_tile, empty)
    extra_scores = (
        jnp.einsum("rhc,rjc->rhj", queries, recent, preferred_element_type=jnp.float32)
        * score_scale
    )
    step_live = jnp.arange(recent.shape[1], dtype=jnp.int32) <= moment
    extra_scores = jnp.where(step_live[None, None, :], extra_scores, -jnp.inf)
    peak = jnp.maximum(jnp.max(scores, axis=2), jnp.max(extra_scores, axis=2))[:, :, None]
    spread = jnp.exp(scores - peak)
    spread_new = jnp.exp(extra_scores - peak)
    softmax_sum = jnp.sum(spread, axis=2, keepdims=True) + jnp.sum(
        spread_new, axis=2, keepdims=True
    )
    weights = (spread / softmax_sum).astype(jnp.bfloat16)
    weights_new = (spread_new / softmax_sum).astype(jnp.bfloat16)
    start_value = jnp.einsum(
        "rhj,rjl->rhl", weights_new, recent[:, :, :LATENT], preferred_element_type=jnp.float32
    )

    def value_tile(tile_index, summed):
        begin_at = tile_index * window
        key_rows = lax.dynamic_slice_in_dim(stored, begin_at, window, 1)[:, :, :LATENT]
        weight_tile = lax.dynamic_slice_in_dim(weights, begin_at, window, 2)
        return summed + jnp.einsum(
            "rht,rtl->rhl", weight_tile, key_rows, preferred_element_type=jnp.float32
        )

    return lax.fori_loop(0, passes, value_tile, start_value).astype(jnp.bfloat16)


def body(q_nope, q_rope, w_absorb_k, w_absorb_v, latent_cache, new_latent, lengths, moves):
    step_count = q_nope.shape[0]
    holders = latent_cache.shape[0]
    capacity = latent_cache.shape[1]
    entries = latent_cache.shape[2]
    movers = moves.shape[1]
    window = min(4 * BLOCK, capacity)
    score_scale = yarn_gain / math.sqrt(HEAD_DIM + ROPE)
    group_count = lax.axis_size("grp")
    column_count = lax.axis_size("head")
    bit_count = group_count.bit_length() - 1
    offsets = moves[0]
    group_here = lax.axis_index("grp")
    column_here = lax.axis_index("head")
    first_slot = (group_here * column_count + column_here) * holders
    counts = lax.dynamic_slice_in_dim(lengths, first_slot, holders)
    source = jnp.mod(group_here - offsets, group_count)
    moved_counts = lengths[
        (source * column_count + column_here) * holders + jnp.arange(movers, dtype=jnp.int32)
    ]
    stored = latent_cache
    recent = jnp.zeros((holders, step_count, entries), jnp.bfloat16)
    results = []
    for moment in range(step_count):
        if moment == 2:
            moving = (stored[:movers], recent[:movers])
            for level in range(bit_count):
                arrived = passed_along((moving[0], moving[1]), "grp", 1 << level)
                chosen = offsets >> level & 1 == 1
                moving = (
                    jnp.where(chosen[:, None, None], arrived[0], moving[0]),
                    jnp.where(chosen[:, None, None], arrived[1], moving[1]),
                )
            stored = jnp.concatenate([moving[0], stored[movers:]], axis=0)
            recent = jnp.concatenate([moving[1], recent[movers:]], axis=0)
            counts = jnp.concatenate([moved_counts, counts[movers:]], axis=0)
        q_latent = jnp.einsum(
            "rhd,hdl->rhl", q_nope[moment], w_absorb_k, preferred_element_type=jnp.float32
        ).astype(jnp.bfloat16)
        query_rows = jnp.concatenate([q_latent, q_rope[moment]], axis=2)
        owned_rows = lax.all_to_all(query_rows, "head", split_axis=0, concat_axis=1, tiled=True)
        fresh_rows = new_latent[moment]
        recent = recent.at[:, moment].set(fresh_rows)
        latent_out = attend(owned_rows, stored, counts, recent, moment, window, score_scale)
        gathered = lax.all_to_all(latent_out, "head", split_axis=1, concat_axis=0, tiled=True)
        results.append(
            jnp.einsum(
                "rhl,hld->rhd", gathered, w_absorb_v, preferred_element_type=jnp.float32
            ).astype(jnp.bfloat16)
        )
    return jnp.stack(results)


def solution(mesh):
    placed = (
        P(None, "grp", "head", None),
        P(None, "grp", "head", None),
        P("head", None, None),
        P("head", None, None),
        P(("grp", "head"), None, None),
        P(None, ("grp", "head"), None),
        P(),
        P("head", None),
    )
    return jax.shard_map(
        body, mesh=mesh, in_specs=placed, out_specs=P(None, "grp", "head", None), check_vma=False
    )
```

profile of v0, /device:TPU:10, one launch (start us, length us, event | category | flops | bytes accessed | tf_op | source)
XLA Modules:
  0.0 180.7 jit_solution(15612328909421631202)
XLA Ops:
  1.0 2.4 %slice.168 = bf16[1,1024,576]{1,2,0:T(8,128)(2,1)} slice(bf16[2,1024,576]{1,2,0:T(8,128)(2,1)} %param.36), slice={[0:1], [0:1024], [0:576]} | slice | bytes 2359296 | tf_op jit(solution)/shard_map/slice | solution.py:95
  3.4 1.6 collective-permute-start.3
  5.1 2.8 %fusion.41 = bf16[8,32,512]{2,0,1:T(8,128)(2,1)S(1)} fusion(bf16[32,128,512]{2,1,0:T(8,128)(2,1)} %param.34, bf16[1,8,32,128]{3,2,1,0:T(8,128)(2,1)S(1)} %get-tuple-element.598), kind=kOutput, calls=%fused_computation.61 | convolution fusion | flops 33685504 | bytes 4521984 | tf_op jit(solution)/shard_map/rhd,hdl->rhl/dot_general | solution.py:106
  8.7 5.3 %all-to-all-start.2 = ((bf16[8,32,576]{2,1,0:T(8,128)(2,1)}), bf16[8,32,576]{2,1,0:T(8,128)(2,1)S(1)}, u32[]{:S(2)}, u32[]{:S(2)}) async-start(bf16[8,32,576]{2,1,0:T(8,128)(2,1)} %copy.84), calls=%async_computation.2 | async-start | bytes 655360 | tf_op jit(solution)/shard_map/all_to_all | solution.py:110
  14.6 2.8 %fusion.42 = bf16[8,32,512]{2,0,1:T(8,128)(2,1)S(1)} fusion(bf16[32,128,512]{2,1,0:T(8,128)(2,1)} %param.34, bf16[1,8,32,128]{3,2,1,0:T(8,128)(2,1)S(1)} %get-tuple-element.597), kind=kOutput, calls=%fused_computation.62 | convolution fusion | flops 33685504 | bytes 4521984 | tf_op jit(solution)/shard_map/rhd,hdl->rhl/dot_general | solution.py:106
  17.4 3.0 %fusion.43 = bf16[8,32,512]{2,0,1:T(8,128)(2,1)S(1)} fusion(bf16[32,128,512]{2,1,0:T(8,128)(2,1)} %param.34, bf16[1,8,32,128]{3,2,1,0:T(8,128)(2,1)S(1)} %get-tuple-element.599), kind=kOutput, calls=%fused_computation.63 | convolution fusion | flops 33685504 | bytes 4521984 | tf_op jit(solution)/shard_map/rhd,hdl->rhl/dot_general | solution.py:106
  25.9 1.5 collective-permute-start.1
  30.5 3.1 %copy.79 = bf16[2,1024,576]{2,1,0:T(8,128)(2,1)S(1)} copy(bf16[2,1024,576]{1,2,0:T(8,128)(2,1)} %param.36) | data formatting | bytes 4718592 | tf_op jit(solution)/shard_map/while | solution.py:67
  33.6 1.7 copy.95
  35.4 1.7 copy.106
  38.5 5.1 %all-to-all-start = ((bf16[8,32,576]{2,1,0:T(8,128)(2,1)}), bf16[8,32,576]{2,1,0:T(8,128)(2,1)}, u32[]{:S(2)}, u32[]{:S(2)}) async-start(bf16[8,32,576]{2,1,0:T(8,128)(2,1)} %copy.73), calls=%async_computation | async-start | bytes 655360 | tf_op jit(solution)/shard_map/all_to_all | solution.py:110
  44.9 2.8 %while.94 = (s32[]{:T(128)}, f32[2,128,1024]{1,2,0:T(8,128)}, s32[]{:T(128)}, s32[2]{0:T(128)S(1)}, bf16[2,1024,576]{1,2,0:T(8,128)(2,1)}, /*index=5*/bf16[2,128...) while((s32[]{:T(128)}, f32[2,128,1024]{1,2,0:T(8,128)}, s32[]{:T(128)}, ...), condition=%wide.region_10.11_spmd.clone, body=%wide.region_9.10_spmd.clone.sunk | while | flops 151258624 | bytes 2006183 | solution.py:40
  44.9 2.8 %fusion.143 = f32[2,128,1024]{1,2,0:T(8,128)} fusion(f32[2,128,1024]{1,2,0:T(8,128)} %get-tuple-element.1027, s32[]{:T(128)S(6)} %select_n.188, bf16[2,128,576]{1,2,0:T(8,128)(2,1)S(1)} %get-tuple-element.1041, bf16[2,1024,576]{1,2,0:T(8,128)(2,1)} %get-tuple-element.1040, pred[2,512]{1,0:T(4,128)(4,1)S(1)} %broadcast_compare_fusion.9), kind=kOutput, calls=%fused_computation.31.clone.1 | convolution fusion | flops 151257088 | bytes 2000896 | tf_op jit(solution)/shard_map/while/body/rhc,rtc->rht/dot_general | solution.py:32
  47.7 3.1 %all-to-all-done = bf16[8,32,576]{2,1,0:T(8,128)(2,1)} async-done(((bf16[8,32,576]{2,1,0:T(8,128)(2,1)}), bf16[8,32,576]{2,1,0:T(8,128)(2,1)}, u32[]{:S(2)}, u32[]{:S(2)}) %all-to-all-start) | async-done | bytes 294944 | tf_op jit(solution)/shard_map/all_to_all | solution.py:110
  50.8 5.6 %all-to-all-start.4 = ((bf16[8,32,576]{2,1,0:T(8,128)(2,1)}), bf16[8,32,576]{2,1,0:T(8,128)(2,1)S(1)}, u32[]{:S(2)}, u32[]{:S(2)}) async-start(bf16[8,32,576]{2,1,0:T(8,128)(2,1)} %copy.95), calls=%async_computation.4 | async-start | bytes 655360 | tf_op jit(solution)/shard_map/all_to_all | solution.py:110
  59.4 2.9 %while.93 = (s32[]{:T(128)}, f32[2,128,1024]{1,2,0:T(8,128)}, s32[]{:T(128)}, s32[2]{0:T(128)S(1)}, bf16[2,1024,576]{1,2,0:T(8,128)(2,1)}, /*index=5*/bf16[2,128...) while((s32[]{:T(128)}, f32[2,128,1024]{1,2,0:T(8,128)}, s32[]{:T(128)}, ...), condition=%wide.region_2.3_spmd.clone, body=%wide.region_1.2_spmd.clone.sunk | while | flops 151258624 | bytes 2006183 | solution.py:40
  59.5 2.8 %fusion.140 = f32[2,128,1024]{1,2,0:T(8,128)} fusion(f32[2,128,1024]{1,2,0:T(8,128)} %get-tuple-element.1084, s32[]{:T(128)S(6)} %select_n.186, bf16[2,128,576]{1,2,0:T(8,128)(2,1)} %get-tuple-element.1098, bf16[2,1024,576]{1,2,0:T(8,128)(2,1)} %get-tuple-element.1097, pred[2,512]{1,0:T(4,128)(4,1)S(1)} %broadcast_compare_fusion.8), kind=kOutput, calls=%fused_computation.23.clone.1 | convolution fusion | flops 151257088 | bytes 2000896 | tf_op jit(solution)/shard_map/while/body/rhc,rtc->rht/dot_general | solution.py:32
  62.3 1.4 reduce_max.100
  65.1 1.4 fusion.53
  67.8 3.0 %broadcast_select_fusion = (bf16[1,1024,576]{1,2,0:T(8,128)(2,1)}, bf16[1,1024,576]{1,2,0:T(8,128)(2,1)}) fusion(bf16[1,1024,576]{1,2,0:T(8,128)(2,1)} %collective-permute-done.3, pred[]{:T(512)} %bitcast.33, bf16[2,1024,576]{1,2,0:T(8,128)(2,1)S(1)} %copy-done.4), kind=kLoop, calls=%fused_computation.57 | loop fusion | flops 589824 | bytes 5898241 | tf_op jit(solution)/shard_map/jit(_where)/select_n | solution.py:100
  70.7 4.4 %collective-permute-start.4 = (bf16[1,1024,576]{1,2,0:T(8,128)(2,1)}, bf16[1,1024,576]{1,2,0:T(8,128)(2,1)}, u32[]{:S(2)}, u32[]{:S(2)}) collective-permute-start(bf16[1,1024,576]{1,2,0:T(8,128)(2,1)} %get-tuple-element.594), channel_id=1, source_target_pairs={{0,8},{4,12},{8,16},{12,20},{16,24},{20,28},{24,0},{28,4},{1,9},{5... | collective-permute-start | bytes 3538952 | tf_op jit(solution)/shard_map/ppermute | solution.py:17
  76.4 1.4 reduce_max.98
  80.3 1.4 fusion.52
  82.6 5.4 %all-to-all-start.6 = ((bf16[8,32,576]{2,1,0:T(8,128)(2,1)}), bf16[8,32,576]{2,1,0:T(8,128)(2,1)}, u32[]{:S(2)}, u32[]{:S(2)}) async-start(bf16[8,32,576]{2,1,0:T(8,128)(2,1)} %copy.106), calls=%async_computation.6 | async-start | bytes 655360 | tf_op jit(solution)/shard_map/all_to_all | solution.py:110
  88.4 9.9 %collective-permute-done.4 = bf16[1,1024,576]{1,2,0:T(8,128)(2,1)} collective-permute-done((bf16[1,1024,576]{1,2,0:T(8,128)(2,1)}, bf16[1,1024,576]{1,2,0:T(8,128)(2,1)}, u32[]{:S(2)}, u32[]{:S(2)}) %collective-permute-start.4) | collective-permute-done | bytes 1179680 | tf_op jit(solution)/shard_map/ppermute | solution.py:17
  98.2 2.4 %broadcast_select_fusion.1 = bf16[1,1024,576]{1,2,0:T(8,128)(2,1)} fusion(bf16[1,1024,576]{1,2,0:T(8,128)(2,1)} %collective-permute-done.4, bf16[1,1024,576]{1,2,0:T(8,128)(2,1)} %get-tuple-element.594, pred[]{:T(512)} %bitcast.32), kind=kLoop, calls=%fused_computation.58 | loop fusion | flops 589824 | bytes 3538945 | tf_op jit(solution)/shard_map/jit(_where)/select_n | solution.py:100
  101.4 4.0 %all-to-all-start.3 = ((bf16[2,128,512]{2,0,1:T(2,128)(2,1)}), bf16[2,128,512]{2,0,1:T(2,128)(2,1)}, u32[]{:S(2)}, u32[]{:S(2)}) async-start(bf16[2,128,512]{2,0,1:T(2,128)(2,1)} %copy.154), calls=%async_computation.3 | async-start | bytes 524288 | tf_op jit(solution)/shard_map/all_to_all | solution.py:114
  105.4 1.4 while.89
  107.9 3.9 %all-to-all-done.3 = bf16[2,128,512]{2,0,1:T(2,128)(2,1)} async-done(((bf16[2,128,512]{2,0,1:T(2,128)(2,1)}), bf16[2,128,512]{2,0,1:T(2,128)(2,1)}, u32[]{:S(2)}, u32[]{:S(2)}) %all-to-all-start.3) | async-done | bytes 262176 | tf_op jit(solution)/shard_map/all_to_all | solution.py:114
  111.8 5.5 %all-to-all-start.1 = ((bf16[2,128,512]{2,0,1:T(2,128)(2,1)}), bf16[2,128,512]{2,0,1:T(2,128)(2,1)S(1)}, u32[]{:S(2)}, u32[]{:S(2)}) async-start(bf16[2,128,512]{2,0,1:T(2,128)(2,1)} %copy.155), calls=%async_computation.1 | async-start | bytes 524288 | tf_op jit(solution)/shard_map/all_to_all | solution.py:114
  121.9 1.7 all-to-all-done.1
  124.7 2.8 %fusion.45 = bf16[1,8,32,128]{3,1,2,0:T(8,128)(2,1)S(1)} fusion(bf16[8,32,512]{2,0,1:T(8,128)(2,1)S(1)} %all_to_all.119, bf16[32,512,128]{2,1,0:T(8,128)(2,1)} %param.35), kind=kOutput, calls=%fused_computation.69 | convolution fusion | flops 33587200 | bytes 4521984 | tf_op jit(solution)/shard_map/rhl,hld->rhd/dot_general | solution.py:116
  127.5 1.5 broadcast_select_fusion.2
  129.5 1.8 while.95
  129.6 1.6 fusion.146
  133.3 2.1 %while.96 = (s32[]{:T(128)}, f32[2,128,1024]{1,2,0:T(8,128)S(1)}, s32[]{:T(128)}, s32[2]{0:T(128)S(1)}, bf16[2,1024,576]{1,2,0:T(8,128)(2,1)}, /*index=5*/bf16[2...) while((s32[]{:T(128)}, f32[2,128,1024]{1,2,0:T(8,128)S(1)}, s32[]{:T(128)}, ...), condition=%wide.region_26.27_spmd.clone, body=%wide.region_25.26_spmd.clone.sunk | while | flops 151258624 | bytes 2007207 | solution.py:40
  133.4 2.0 %fusion.149 = f32[2,128,1024]{1,2,0:T(8,128)S(1)} fusion(f32[2,128,1024]{1,2,0:T(8,128)S(1)} %get-tuple-element.913, s32[]{:T(128)S(6)} %select_n.192, bf16[2,128,576]{1,2,0:T(8,128)(2,1)} %get-tuple-element.927, bf16[2,1024,576]{1,2,0:T(8,128)(2,1)} %get-tuple-element.926, pred[2,512]{1,0:T(4,128)(4,1)S(1)} %broadcast_compare_fusion.11), kind=kOutput, calls=%fused_computation.47.clone.1 | convolution fusion | flops 151257088 | bytes 2001920 | tf_op jit(solution)/shard_map/while/body/rhc,rtc->rht/dot_general | solution.py:32
  138.2 3.1 %copy.101 = bf16[2,1024,576]{2,1,0:T(8,128)(2,1)S(1)} copy(bf16[2,1024,576]{1,2,0:T(8,128)(2,1)} %get-tuple-element.1135) | data formatting | bytes 4718592 | tf_op jit(solution)/shard_map/while | solution.py:67
  141.3 2.2 %divide_convert_fusion.1 = bf16[2,128,1024]{1,2,0:T(8,128)(2,1)} fusion(f32[2,128,1024]{1,2,0:T(8,128)} %copy-done.3, f32[2,128]{1,0:T(2,128)S(1)} %add.192, f32[2,128]{1,0:T(2,128)S(1)} %max.30), kind=kLoop, calls=%fused_computation.82 | loop fusion | flops 786432 | bytes 1574912 | tf_op jit(solution)/shard_map/convert_element_type | solution.py:53
  143.5 2.3 %while.92 = (s32[]{:T(128)}, f32[2,128,512]{2,1,0:T(8,128)}, s32[]{:T(128)}, bf16[2,128,1024]{1,2,0:T(8,128)(2,1)}, bf16[2,1024,576]{2,1,0:T(8,128)(2,1)S(1)}, /*index=5*/s32[]{:T(128)}, s32[]{:T(128)}, s32[]{:T(128)}, s32[]{:T(128)}) while((s32[]{:T(128)}, f32[2,128,512]{2,1,0:T(8,128)}, s32[]{:T(128)}, bf16[2,128,1024]{1,2,0:T(8,128)(2,1)}, ...), condition=%wide.region_32.33_spmd, body=%wide.region_31.32_spmd.sunk | while | flops 134348800 | bytes 2360467 | solution.py:67
  143.5 2.3 %convolution_add_fusion.11 = f32[2,128,512]{2,1,0:T(8,128)} fusion(f32[2,128,512]{2,1,0:T(8,128)} %get-tuple-element.942, bf16[2,1024,576]{2,1,0:T(8,128)(2,1)S(1)} %get-tuple-element.954, s32[]{:T(128)S(6)} %select_n.184, bf16[2,128,1024]{1,2,0:T(8,128)(2,1)} %get-tuple-element.953), kind=kOutput, calls=%fused_computation.16.clone.1 | convolution fusion | flops 134348800 | bytes 2360320 | tf_op jit(solution)/shard_map/while/body/rht,rtl->rhl/dot_general | solution.py:63
  145.7 2.1 %copy.152 = bf16[2,128,512]{2,0,1:T(2,128)(2,1)} copy(f32[2,128,512]{2,1,0:T(8,128)} %get-tuple-element.324) | data formatting | bytes 786432 | tf_op jit(solution)/shard_map/while | solution.py:67
  147.9 11.7 %all-to-all-start.7 = ((bf16[2,128,512]{2,0,1:T(2,128)(2,1)}), bf16[2,128,512]{2,0,1:T(2,128)(2,1)}, u32[]{:S(2)}, u32[]{:S(2)}) async-start(bf16[2,128,512]{2,0,1:T(2,128)(2,1)} %copy.152), calls=%async_computation.7 | async-start | bytes 524288 | tf_op jit(solution)/shard_map/all_to_all | solution.py:114
  162.0 3.8 %all-to-all-done.7 = bf16[2,128,512]{2,0,1:T(2,128)(2,1)} async-done(((bf16[2,128,512]{2,0,1:T(2,128)(2,1)}), bf16[2,128,512]{2,0,1:T(2,128)(2,1)}, u32[]{:S(2)}, u32[]{:S(2)}) %all-to-all-start.7) | async-done | bytes 262176 | tf_op jit(solution)/shard_map/all_to_all | solution.py:114
  165.9 4.0 %all-to-all-start.5 = ((bf16[2,128,512]{2,0,1:T(2,128)(2,1)}), bf16[2,128,512]{2,0,1:T(2,128)(2,1)S(1)}, u32[]{:S(2)}, u32[]{:S(2)}) async-start(bf16[2,128,512]{2,0,1:T(2,128)(2,1)} %copy.153), calls=%async_computation.5 | async-start | bytes 524288 | tf_op jit(solution)/shard_map/all_to_all | solution.py:114
  169.9 2.8 %fusion.44 = bf16[1,8,32,128]{3,1,2,0:T(8,128)(2,1)S(1)} fusion(bf16[8,32,512]{2,0,1:T(8,128)(2,1)S(1)} %copy-done.11, bf16[32,512,128]{2,1,0:T(8,128)(2,1)} %param.35), kind=kOutput, calls=%fused_computation.68 | convolution fusion | flops 33587200 | bytes 4521984 | tf_op jit(solution)/shard_map/rhl,hld->rhd/dot_general | solution.py:116
  173.9 2.8 %fusion.47 = bf16[1,8,32,128]{3,1,2,0:T(8,128)(2,1)S(1)} fusion(bf16[8,32,512]{2,0,1:T(8,128)(2,1)S(1)} %all_to_all.135, bf16[32,512,128]{2,1,0:T(8,128)(2,1)} %param.35), kind=kOutput, calls=%fused_computation.71 | convolution fusion | flops 33587200 | bytes 4521984 | tf_op jit(solution)/shard_map/rhl,hld->rhd/dot_general | solution.py:116
  177.1 2.8 %fusion.46 = bf16[1,8,32,128]{3,1,2,0:T(8,128)(2,1)S(1)} fusion(bf16[8,32,512]{2,0,1:T(8,128)(2,1)S(1)} %all_to_all.127, bf16[32,512,128]{2,1,0:T(8,128)(2,1)} %param.35), kind=kOutput, calls=%fused_computation.70 | convolution fusion | flops 33587200 | bytes 4521984 | tf_op jit(solution)/shard_map/rhl,hld->rhd/dot_general | solution.py:116
  (143 shorter events, 43.3 us)
Async XLA Ops:
  0.0 5.0 %copy-start.12 = (bf16[4,8,32,64]{3,2,1,0:T(8,128)(2,1)S(1)}, bf16[4,8,32,64]{3,2,1,0:T(8,128)(2,1)}, u32[]{:S(2)}) copy-start(bf16[4,8,32,64]{3,2,1,0:T(8,128)(2,1)} %param.33) | copy-start | bytes 393220
  0.0 5.0 %copy-start.13 = (bf16[4,8,32,128]{3,2,1,0:T(8,128)(2,1)S(1)}, bf16[4,8,32,128]{3,2,1,0:T(8,128)(2,1)}, u32[]{:S(2)}) copy-start(bf16[4,8,32,128]{3,2,1,0:T(8,128)(2,1)} %param.32) | copy-start | bytes 786436
  0.9 24.9 %collective-permute-start = (bf16[1,4,576]{2,1,0:T(4,128)(2,1)S(1)}, bf16[1,4,576]{2,1,0:T(4,128)(2,1)S(1)}, u32[]{:S(2)}, u32[]{:S(2)}) collective-permute-start(bf16[1,4,576]{2,1,0:T(4,128)(2,1)S(1)} %slice.181), channel_id=1, source_target_pairs={{0,4},{4,8},{8,12},{12,16},{16,20},{20,24},{24,28},{28,0},{1,5},{5... | collective-permute-start | bytes 13832 | tf_op jit(solution)/shard_map/ppermute | solution.py:17
  3.4 64.4 %collective-permute-start.3 = (bf16[1,1024,576]{1,2,0:T(8,128)(2,1)}, bf16[1,1024,576]{1,2,0:T(8,128)(2,1)}, u32[]{:S(2)}, u32[]{:S(2)}) collective-permute-start(bf16[1,1024,576]{1,2,0:T(8,128)(2,1)} %slice.168), channel_id=1, source_target_pairs={{0,4},{4,8},{8,12},{12,16},{16,20},{20,24},{24,28},{28,0},{1,5},{5... | collective-permute-start | bytes 3538952 | tf_op jit(solution)/shard_map/ppermute | solution.py:17
  8.7 29.7 %all-to-all-start.2 = ((bf16[8,32,576]{2,1,0:T(8,128)(2,1)}), bf16[8,32,576]{2,1,0:T(8,128)(2,1)S(1)}, u32[]{:S(2)}, u32[]{:S(2)}) async-start(bf16[8,32,576]{2,1,0:T(8,128)(2,1)} %copy.84), calls=%async_computation.2 | async-start | bytes 655360 | tf_op jit(solution)/shard_map/all_to_all | solution.py:110
  17.4 3.5 %copy-start = (bf16[32,128,512]{2,1,0:T(8,128)(2,1)S(1)}, bf16[32,128,512]{2,1,0:T(8,128)(2,1)}, u32[]{:S(2)}) copy-start(bf16[32,128,512]{2,1,0:T(8,128)(2,1)} %param.34) | copy-start | bytes 12582916
  20.9 2.3 %copy-start.14 = (s32[64]{0:T(128)S(1)}, s32[64]{0:T(128)}, u32[]{:S(2)}) copy-start(s32[64]{0:T(128)} %param.38) | copy-start | bytes 772
  25.9 12.0 %collective-permute-start.1 = (bf16[1,4,576]{2,1,0:T(4,128)(2,1)S(1)}, bf16[1,4,576]{2,1,0:T(4,128)(2,1)S(1)}, u32[]{:S(2)}, u32[]{:S(2)}) collective-permute-start(bf16[1,4,576]{2,1,0:T(4,128)(2,1)S(1)} %get-tuple-element.608), channel_id=1, source_target_pairs={{0,8},{4,12},{8,16},{12,20},{16,24},{20,28},{24,0},{28,4},{1,9},{5... | collective-permute-start | bytes 13832 | tf_op jit(solution)/shard_map/ppermute | solution.py:17
  37.9 79.5 %collective-permute-start.2 = (bf16[1,4,576]{2,1,0:T(4,128)(2,1)S(1)}, bf16[1,4,576]{2,1,0:T(4,128)(2,1)S(1)}, u32[]{:S(2)}, u32[]{:S(2)}) collective-permute-start(bf16[1,4,576]{2,1,0:T(4,128)(2,1)S(1)} %broadcast_select_fusion.4), channel_id=1, source_target_pairs={{0,16},{4,20},{8,24},{12,28},{16,0},{20,4},{24,8},{28,12},{1,17},{... | collective-permute-start | bytes 13832 | tf_op jit(solution)/shard_map/ppermute | solution.py:17
  38.5 12.4 %all-to-all-start = ((bf16[8,32,576]{2,1,0:T(8,128)(2,1)}), bf16[8,32,576]{2,1,0:T(8,128)(2,1)}, u32[]{:S(2)}, u32[]{:S(2)}) async-start(bf16[8,32,576]{2,1,0:T(8,128)(2,1)} %copy.73), calls=%async_computation | async-start | bytes 655360 | tf_op jit(solution)/shard_map/all_to_all | solution.py:110
  43.6 1.3 copy-start.10
  50.8 31.8 %all-to-all-start.4 = ((bf16[8,32,576]{2,1,0:T(8,128)(2,1)}), bf16[8,32,576]{2,1,0:T(8,128)(2,1)S(1)}, u32[]{:S(2)}, u32[]{:S(2)}) async-start(bf16[8,32,576]{2,1,0:T(8,128)(2,1)} %copy.95), calls=%async_computation.4 | async-start | bytes 655360 | tf_op jit(solution)/shard_map/all_to_all | solution.py:110
  57.4 2.0 %copy-start.9 = (bf16[4,2,32,576]{3,2,0,1:T(8,128)(2,1)}, bf16[4,2,32,576]{3,2,0,1:T(8,128)(2,1)S(1)}, u32[]{:S(2)}) copy-start(bf16[4,2,32,576]{3,2,0,1:T(8,128)(2,1)S(1)} %copy.74) | copy-start | bytes 884740
  59.4 4.3 %copy-start.15 = (pred[4]{0:T(512)(128)(4,1)S(1)}, pred[4]{0:T(512)(128)(4,1)}, u32[]{:S(2)}) copy-start(pred[4]{0:T(512)(128)(4,1)} %iota_compare_fusion.2) | copy-start | bytes 16
  63.7 3.1 %copy-start.1 = (f32[2,128,1024]{1,2,0:T(8,128)S(1)}, f32[2,128,1024]{1,2,0:T(8,128)}, u32[]{:S(2)}) copy-start(f32[2,128,1024]{1,2,0:T(8,128)} %get-tuple-element.319) | copy-start | bytes 3145732
  63.7 4.1 %copy-start.4 = (bf16[2,1024,576]{1,2,0:T(8,128)(2,1)S(1)}, bf16[2,1024,576]{1,2,0:T(8,128)(2,1)}, u32[]{:S(2)}) copy-start(bf16[2,1024,576]{1,2,0:T(8,128)(2,1)} %get-tuple-element.1133) | copy-start | bytes 7077892
  70.7 27.5 %collective-permute-start.4 = (bf16[1,1024,576]{1,2,0:T(8,128)(2,1)}, bf16[1,1024,576]{1,2,0:T(8,128)(2,1)}, u32[]{:S(2)}, u32[]{:S(2)}) collective-permute-start(bf16[1,1024,576]{1,2,0:T(8,128)(2,1)} %get-tuple-element.594), channel_id=1, source_target_pairs={{0,8},{4,12},{8,16},{12,20},{16,24},{20,28},{24,0},{28,4},{1,9},{5... | collective-permute-start | bytes 3538952 | tf_op jit(solution)/shard_map/ppermute | solution.py:17
  77.8 3.8 %copy-start.2 = (f32[2,128,1024]{1,2,0:T(8,128)S(1)}, f32[2,128,1024]{1,2,0:T(8,128)}, u32[]{:S(2)}) copy-start(f32[2,128,1024]{1,2,0:T(8,128)} %get-tuple-element.317) | copy-start | bytes 3145732
  82.6 18.7 %all-to-all-start.6 = ((bf16[8,32,576]{2,1,0:T(8,128)(2,1)}), bf16[8,32,576]{2,1,0:T(8,128)(2,1)}, u32[]{:S(2)}, u32[]{:S(2)}) async-start(bf16[8,32,576]{2,1,0:T(8,128)(2,1)} %copy.106), calls=%async_computation.6 | async-start | bytes 655360 | tf_op jit(solution)/shard_map/all_to_all | solution.py:110
  100.7 26.9 %collective-permute-start.5 = (bf16[1,1024,576]{1,2,0:T(8,128)(2,1)}, bf16[1,1024,576]{1,2,0:T(8,128)(2,1)}, u32[]{:S(2)}, u32[]{:S(2)}) collective-permute-start(bf16[1,1024,576]{1,2,0:T(8,128)(2,1)} %broadcast_select_fusion.1), channel_id=1, source_target_pairs={{0,16},{4,20},{8,24},{12,28},{16,0},{20,4},{24,8},{28,12},{1,17},{... | collective-permute-start | bytes 3538952 | tf_op jit(solution)/shard_map/ppermute | solution.py:17
  101.4 10.4 %all-to-all-start.3 = ((bf16[2,128,512]{2,0,1:T(2,128)(2,1)}), bf16[2,128,512]{2,0,1:T(2,128)(2,1)}, u32[]{:S(2)}, u32[]{:S(2)}) async-start(bf16[2,128,512]{2,0,1:T(2,128)(2,1)} %copy.154), calls=%async_computation.3 | async-start | bytes 524288 | tf_op jit(solution)/shard_map/all_to_all | solution.py:114
  111.8 11.9 %all-to-all-start.1 = ((bf16[2,128,512]{2,0,1:T(2,128)(2,1)}), bf16[2,128,512]{2,0,1:T(2,128)(2,1)S(1)}, u32[]{:S(2)}, u32[]{:S(2)}) async-start(bf16[2,128,512]{2,0,1:T(2,128)(2,1)} %copy.155), calls=%async_computation.1 | async-start | bytes 524288 | tf_op jit(solution)/shard_map/all_to_all | solution.py:114
  119.6 7.9 %copy-start.7 = (bf16[4,2,32,576]{3,2,0,1:T(8,128)(2,1)}, bf16[4,2,32,576]{3,2,0,1:T(8,128)(2,1)S(1)}, u32[]{:S(2)}) copy-start(bf16[4,2,32,576]{3,2,0,1:T(8,128)(2,1)S(1)} %copy.107) | copy-start | bytes 884740
  127.5 1.6 copy-start.6
  131.2 1.0 copy-start.3
  131.2 1.7 copy-start.5
  133.3 2.2 %copy-start.8 = (bf16[4,2,32,576]{3,2,0,1:T(8,128)(2,1)S(1)}, bf16[4,2,32,576]{3,2,0,1:T(8,128)(2,1)}, u32[]{:S(2)}) copy-start(bf16[4,2,32,576]{3,2,0,1:T(8,128)(2,1)} %copy-done.7) | copy-start | bytes 884740
  147.9 18.0 %all-to-all-start.7 = ((bf16[2,128,512]{2,0,1:T(2,128)(2,1)}), bf16[2,128,512]{2,0,1:T(2,128)(2,1)}, u32[]{:S(2)}, u32[]{:S(2)}) async-start(bf16[2,128,512]{2,0,1:T(2,128)(2,1)} %copy.152), calls=%async_computation.7 | async-start | bytes 524288 | tf_op jit(solution)/shard_map/all_to_all | solution.py:114
  159.5 10.3 %copy-start.11 = (bf16[8,32,512]{2,0,1:T(8,128)(2,1)S(1)}, bf16[8,32,512]{2,0,1:T(8,128)(2,1)}, u32[]{:S(2)}) copy-start(bf16[8,32,512]{2,0,1:T(8,128)(2,1)} %all_to_all.111) | copy-start | bytes 786436
  165.9 10.9 %all-to-all-start.5 = ((bf16[2,128,512]{2,0,1:T(2,128)(2,1)}), bf16[2,128,512]{2,0,1:T(2,128)(2,1)S(1)}, u32[]{:S(2)}, u32[]{:S(2)}) async-start(bf16[2,128,512]{2,0,1:T(2,128)(2,1)} %copy.153), calls=%async_computation.5 | async-start | bytes 524288 | tf_op jit(solution)/shard_map/all_to_all | solution.py:114
where the time goes:
time: 183 us; the launch traced here: 181 us
  starting transfers between devices  55.5 us (30%)
  matrix products  41.1 us (22%)
  local copies, waits for them, and re-layouts  35.3 us (19%)
  other arithmetic  23 us (13%)
  waiting for transfers between devices  22.5 us (12%)
  between operations  3.04 us (2%)
    all_to_all x4, starting transfers between devices, body(): lax.all_to_all(latent_out, 'head', split_axis=1, concat_axis=0, tiled=True)  25.2 us
    all_to_all x4, starting transfers between devices, body(): lax.all_to_all(query_rows, 'head', split_axis=0, concat_axis=1, tiled=True)  21.5 us
    while x6, local copies, waits for them, and re-layouts, attend(): lax.fori_loop(0, passes, value_tile, start_value).astype(jnp.bfloat16)  11.7 us
    dot_general x4, matrix products, body(): jnp.einsum('rhl,hld->rhd', gathered, w_absorb_v, preferred_element_type=j...  11.3 us
    ppermute x6, waiting for transfers between devices, passed_along(): return lax.ppermute(value, axis, pairs)  9.89 us
    all_to_all x4, waiting for transfers between devices, body(): lax.all_to_all(latent_out, 'head', split_axis=1, concat_axis=0, tiled=True)  9.49 us
    dot_general x4, matrix products, body(): jnp.einsum('rhd,hdl->rhl', q_nope[moment], w_absorb_k, preferred_element_...  9.29 us
    dot_general x4, matrix products, score_tile(): jnp.einsum('rhc,rtc->rht', queries, key_rows, preferred_element_type=jnp....  9.25 us
  transfers between devices with their start and end apart: 14, of which 5 were waited for; matrix products, arithmetic and copies ran while one was open for 40% of the time, Pallas kernels for 0%

commit v1 on v0

--- a/solution.py
+++ b/solution.py
@@ -111,7 +111,12 @@
         fresh_rows = new_latent[moment]
         recent = recent.at[:, moment].set(fresh_rows)
         latent_out = attend(owned_rows, stored, counts, recent, moment, window, score_scale)
-        gathered = lax.all_to_all(latent_out, "head", split_axis=1, concat_axis=0, tiled=True)
+        gathered = jnp.concatenate(
+            lax.all_to_all(
+                jnp.stack(jnp.split(latent_out, lax.axis_size("head"), axis=1)), "head", 0, 0
+            ),
+            axis=0,
+        )
         results.append(
             jnp.einsum(
                 "rhl,hld->rhd", gathered, w_absorb_v, preferred_element_type=jnp.float32

time: 183 us -> 191 us (1.044)
  the two profiles are of different devices: /device:TPU:10 before, /device:TPU:0 now
where the time goes in v1:
time: 191 us; the launch traced here: 189 us
  starting transfers between devices  68.3 us (36%)
  matrix products  37.8 us (20%)
  other arithmetic  28.6 us (15%)
  local copies, waits for them, and re-layouts  27.7 us (15%)
  waiting for transfers between devices  22.9 us (12%)
  between operations  3.03 us (2%)
    all_to_all x4, starting transfers between devices, body(): lax.all_to_all(jnp.stack(jnp.split(latent_out, lax.axis_size('head'), axi...  31.4 us
    all_to_all x4, starting transfers between devices, body(): lax.all_to_all(query_rows, 'head', split_axis=0, concat_axis=1, tiled=True)  27 us
    all_to_all x4, waiting for transfers between devices, body(): lax.all_to_all(jnp.stack(jnp.split(latent_out, lax.axis_size('head'), axi...  12.9 us
    ppermute x6, waiting for transfers between devices, passed_along(): return lax.ppermute(value, axis, pairs)  9.97 us
    ppermute x6, starting transfers between devices, passed_along(): return lax.ppermute(value, axis, pairs)  9.92 us
    dot_general x4, matrix products, body(): jnp.einsum('rhl,hld->rhd', gathered, w_absorb_v, preferred_element_type=j...  9.66 us
    dot_general x4, matrix products, score_tile(): jnp.einsum('rhc,rtc->rht', queries, key_rows, preferred_element_type=jnp....  9.22 us
    dot_general x4, matrix products, value_tile(): jnp.einsum('rht,rtl->rhl', weight_tile, key_rows, preferred_element_type=...  7.19 us
  transfers between devices with their start and end apart: 14, of which 6 were waited for; matrix products, arithmetic and copies ran while one was open for 46% of the time, Pallas kernels for 0%

profile of v1, /device:TPU:0, one launch (start us, length us, event | category | flops | bytes accessed | tf_op | source)
XLA Modules:
  0.0 188.5 jit_solution(1445391300458256755)
XLA Ops:
  1.5 2.4 %slice.168 = bf16[1,1024,576]{1,2,0:T(8,128)(2,1)} slice(bf16[2,1024,576]{1,2,0:T(8,128)(2,1)} %param.36), slice={[0:1], [0:1024], [0:576]} | slice | bytes 2359296 | tf_op jit(solution)/shard_map/slice | solution.py:95
  3.8 2.6 %collective-permute-start.3 = (bf16[1,1024,576]{1,2,0:T(8,128)(2,1)}, bf16[1,1024,576]{1,2,0:T(8,128)(2,1)}, u32[]{:S(2)}, u32[]{:S(2)}) collective-permute-start(bf16[1,1024,576]{1,2,0:T(8,128)(2,1)} %slice.168), channel_id=1, source_target_pairs={{0,4},{4,8},{8,12},{12,16},{16,20},{20,24},{24,28},{28,0},{1,5},{5... | collective-permute-start | bytes 3538952 | tf_op jit(solution)/shard_map/ppermute | solution.py:17
  6.6 2.8 %fusion.41 = bf16[8,32,512]{2,0,1:T(8,128)(2,1)S(1)} fusion(bf16[32,128,512]{2,1,0:T(8,128)(2,1)} %param.34, bf16[1,8,32,128]{3,2,1,0:T(8,128)(2,1)S(1)} %get-tuple-element.602), kind=kOutput, calls=%fused_computation.61 | convolution fusion | flops 33685504 | bytes 4521984 | tf_op jit(solution)/shard_map/rhd,hdl->rhl/dot_general | solution.py:106
  10.2 4.9 %all-to-all-start.2 = ((bf16[8,32,576]{2,1,0:T(8,128)(2,1)}), bf16[8,32,576]{2,1,0:T(8,128)(2,1)S(1)}, u32[]{:S(2)}, u32[]{:S(2)}) async-start(bf16[8,32,576]{2,1,0:T(8,128)(2,1)} %copy.83), calls=%async_computation.2 | async-start | bytes 655360 | tf_op jit(solution)/shard_map/all_to_all | solution.py:110
  15.1 3.0 %fusion.42 = bf16[8,32,512]{2,0,1:T(8,128)(2,1)S(1)} fusion(bf16[32,128,512]{2,1,0:T(8,128)(2,1)} %param.34, bf16[1,8,32,128]{3,2,1,0:T(8,128)(2,1)S(1)} %get-tuple-element.601), kind=kOutput, calls=%fused_computation.62 | convolution fusion | flops 33685504 | bytes 4521984 | tf_op jit(solution)/shard_map/rhd,hdl->rhl/dot_general | solution.py:106
  22.1 1.5 collective-permute-start.1
  26.7 1.6 collective-permute-start.2
  31.5 3.1 %copy.79 = bf16[2,1024,576]{2,1,0:T(8,128)(2,1)S(1)} copy(bf16[2,1024,576]{1,2,0:T(8,128)(2,1)} %param.36) | data formatting | bytes 4718592 | tf_op jit(solution)/shard_map/while | solution.py:67
  34.6 1.7 copy.93
  36.3 1.7 copy.103
  38.9 5.1 %all-to-all-start = ((bf16[8,32,576]{2,1,0:T(8,128)(2,1)}), bf16[8,32,576]{2,1,0:T(8,128)(2,1)S(1)}, u32[]{:S(2)}, u32[]{:S(2)}) async-start(bf16[8,32,576]{2,1,0:T(8,128)(2,1)} %copy.73), calls=%async_computation | async-start | bytes 655360 | tf_op jit(solution)/shard_map/all_to_all | solution.py:110
  48.2 2.8 %while.94 = (s32[]{:T(128)}, f32[2,128,1024]{1,2,0:T(8,128)}, s32[]{:T(128)}, s32[2]{0:T(128)S(1)}, bf16[2,1024,576]{1,2,0:T(8,128)(2,1)}, /*index=5*/bf16[2,128...) while((s32[]{:T(128)}, f32[2,128,1024]{1,2,0:T(8,128)}, s32[]{:T(128)}, ...), condition=%wide.region_10.11_spmd.clone, body=%wide.region_9.10_spmd.clone.sunk | while | flops 151258624 | bytes 2006183 | solution.py:40
  48.3 2.8 %fusion.143 = f32[2,128,1024]{1,2,0:T(8,128)} fusion(f32[2,128,1024]{1,2,0:T(8,128)} %get-tuple-element.1043, s32[]{:T(128)S(6)} %select_n.188, bf16[2,128,576]{1,2,0:T(8,128)(2,1)S(1)} %get-tuple-element.1057, bf16[2,1024,576]{1,2,0:T(8,128)(2,1)} %get-tuple-element.1056, pred[2,512]{1,0:T(4,128)(4,1)S(1)} %broadcast_compare_fusion.9), kind=kOutput, calls=%fused_computation.31.clone.1 | convolution fusion | flops 151257088 | bytes 2000896 | tf_op jit(solution)/shard_map/while/body/rhc,rtc->rht/dot_general | solution.py:32
  51.1 1.4 reduce_max.100
  52.5 1.4 fusion.53
  53.9 2.2 %divide_convert_fusion.2 = bf16[2,128,1024]{1,2,0:T(8,128)(2,1)} fusion(f32[2,128,1024]{1,2,0:T(8,128)} %get-tuple-element.319, f32[2,128]{1,0:T(2,128)S(1)} %add.187, f32[2,128]{1,0:T(2,128)S(1)} %max.29), kind=kLoop, calls=%fused_computation.84 | loop fusion | flops 786432 | bytes 1574912 | tf_op jit(solution)/shard_map/convert_element_type | solution.py:53
  56.8 7.9 %all-to-all-start.4 = ((bf16[8,32,576]{2,1,0:T(8,128)(2,1)}), bf16[8,32,576]{2,1,0:T(8,128)(2,1)S(1)}, u32[]{:S(2)}, u32[]{:S(2)}) async-start(bf16[8,32,576]{2,1,0:T(8,128)(2,1)} %copy.93), calls=%async_computation.4 | async-start | bytes 655360 | tf_op jit(solution)/shard_map/all_to_all | solution.py:110
  67.9 2.9 %while.93 = (s32[]{:T(128)}, f32[2,128,1024]{1,2,0:T(8,128)}, s32[]{:T(128)}, s32[2]{0:T(128)S(1)}, bf16[2,1024,576]{1,2,0:T(8,128)(2,1)}, /*index=5*/bf16[2,128...) while((s32[]{:T(128)}, f32[2,128,1024]{1,2,0:T(8,128)}, s32[]{:T(128)}, ...), condition=%wide.region_2.3_spmd.clone, body=%wide.region_1.2_spmd.clone.sunk | while | flops 151258624 | bytes 2006183 | solution.py:40
  68.0 2.8 %fusion.140 = f32[2,128,1024]{1,2,0:T(8,128)} fusion(f32[2,128,1024]{1,2,0:T(8,128)} %get-tuple-element.1100, s32[]{:T(128)S(6)} %select_n.186, bf16[2,128,576]{1,2,0:T(8,128)(2,1)} %get-tuple-element.1114, bf16[2,1024,576]{1,2,0:T(8,128)(2,1)} %get-tuple-element.1113, pred[2,512]{1,0:T(4,128)(4,1)S(1)} %broadcast_compare_fusion.8), kind=kOutput, calls=%fused_computation.23.clone.1 | convolution fusion | flops 151257088 | bytes 2000896 | tf_op jit(solution)/shard_map/while/body/rhc,rtc->rht/dot_general | solution.py:32
  70.8 1.4 reduce_max.98
  72.2 1.4 fusion.52
  73.6 2.2 %divide_convert_fusion.3 = bf16[2,128,1024]{1,2,0:T(8,128)(2,1)} fusion(f32[2,128,1024]{1,2,0:T(8,128)} %get-tuple-element.317, f32[2,128]{1,0:T(2,128)S(1)} %add.186, f32[2,128]{1,0:T(2,128)S(1)} %max.28), kind=kLoop, calls=%fused_computation.86 | loop fusion | flops 786432 | bytes 1574912 | tf_op jit(solution)/shard_map/convert_element_type | solution.py:53
  77.4 3.6 %broadcast_select_fusion = (bf16[1,1024,576]{1,2,0:T(8,128)(2,1)}, bf16[1,1024,576]{1,2,0:T(8,128)(2,1)}) fusion(bf16[1,1024,576]{1,2,0:T(8,128)(2,1)} %collective-permute-done.3, pred[]{:T(512)} %bitcast.39, bf16[2,1024,576]{1,2,0:T(8,128)(2,1)} %get-tuple-element.1149), kind=kLoop, calls=%fused_computation.57 | loop fusion | flops 589824 | bytes 5898241 | tf_op jit(solution)/shard_map/jit(_where)/select_n | solution.py:100
  81.0 2.2 %collective-permute-start.4 = (bf16[1,1024,576]{1,2,0:T(8,128)(2,1)}, bf16[1,1024,576]{1,2,0:T(8,128)(2,1)}, u32[]{:S(2)}, u32[]{:S(2)}) collective-permute-start(bf16[1,1024,576]{1,2,0:T(8,128)(2,1)} %get-tuple-element.594), channel_id=1, source_target_pairs={{0,8},{4,12},{8,16},{12,20},{16,24},{20,28},{24,0},{28,4},{1,9},{5... | collective-permute-start | bytes 3538952 | tf_op jit(solution)/shard_map/ppermute | solution.py:17
  84.3 2.3 %while.89 = (s32[]{:T(128)}, f32[2,128,512]{2,1,0:T(8,128)}, s32[]{:T(128)}, bf16[2,128,1024]{1,2,0:T(8,128)(2,1)}, bf16[2,1024,576]{2,1,0:T(8,128)(2,1)S(1)}, /*index=5*/s32[]{:T(128)}, s32[]{:T(128)}, s32[]{:T(128)}, s32[]{:T(128)}) while((s32[]{:T(128)}, f32[2,128,512]{2,1,0:T(8,128)}, s32[]{:T(128)}, bf16[2,128,1024]{1,2,0:T(8,128)(2,1)}, ...), condition=%wide.region_8.9_spmd, body=%wide.region_7.8_spmd.sunk | while | flops 134348800 | bytes 2360467 | solution.py:67
  84.3 2.3 %convolution_add_fusion.8 = f32[2,128,512]{2,1,0:T(8,128)} fusion(f32[2,128,512]{2,1,0:T(8,128)} %get-tuple-element.1129, bf16[2,1024,576]{2,1,0:T(8,128)(2,1)S(1)} %get-tuple-element.1141, s32[]{:T(128)S(6)} %select_n.181, bf16[2,128,1024]{1,2,0:T(8,128)(2,1)} %get-tuple-element.1140), kind=kOutput, calls=%fused_computation.4.clone.1 | convolution fusion | flops 134348800 | bytes 2360320 | tf_op jit(solution)/shard_map/while/body/rht,rtl->rhl/dot_general | solution.py:63
  87.7 9.1 %all-to-all-start.6 = ((bf16[8,32,576]{2,1,0:T(8,128)(2,1)}), bf16[8,32,576]{2,1,0:T(8,128)(2,1)S(1)}, u32[]{:S(2)}, u32[]{:S(2)}) async-start(bf16[8,32,576]{2,1,0:T(8,128)(2,1)} %copy.103), calls=%async_computation.6 | async-start | bytes 655360 | tf_op jit(solution)/shard_map/all_to_all | solution.py:110
  96.8 8.8 %collective-permute-done.4 = bf16[1,1024,576]{1,2,0:T(8,128)(2,1)} collective-permute-done((bf16[1,1024,576]{1,2,0:T(8,128)(2,1)}, bf16[1,1024,576]{1,2,0:T(8,128)(2,1)}, u32[]{:S(2)}, u32[]{:S(2)}) %collective-permute-start.4) | collective-permute-done | bytes 1179680 | tf_op jit(solution)/shard_map/ppermute | solution.py:17
  105.6 1.4 broadcast_select_fusion.1
  107.0 1.5 collective-permute-start.5
  109.2 7.7 %all-to-all-start.3 = ((bf16[4,2,32,512]{3,2,1,0:T(8,128)(2,1)}), bf16[4,2,32,512]{3,2,1,0:T(8,128)(2,1)S(1)}, u32[]{:S(2)}, u32[]{:S(2)}) async-start(bf16[4,2,32,512]{3,2,1,0:T(8,128)(2,1)} %pad_maximum_fusion.6), calls=%async_computation.3 | async-start | bytes 524288 | tf_op jit(solution)/shard_map/all_to_all | solution.py:115
  119.8 3.9 %all-to-all-done.3 = bf16[4,2,32,512]{3,2,1,0:T(8,128)(2,1)S(1)} async-done(((bf16[4,2,32,512]{3,2,1,0:T(8,128)(2,1)}), bf16[4,2,32,512]{3,2,1,0:T(8,128)(2,1)S(1)}, u32[]{:S(2)}, u32[]{:S(2)}) %all-to-all-start.3) | async-done | bytes 262176 | tf_op jit(solution)/shard_map/all_to_all | solution.py:115
  123.7 4.0 %all-to-all-start.1 = ((bf16[4,2,32,512]{3,2,1,0:T(8,128)(2,1)}), bf16[4,2,32,512]{3,2,1,0:T(8,128)(2,1)}, u32[]{:S(2)}, u32[]{:S(2)}) async-start(bf16[4,2,32,512]{3,2,1,0:T(8,128)(2,1)} %pad_maximum_fusion.5), calls=%async_computation.1 | async-start | bytes 524288 | tf_op jit(solution)/shard_map/all_to_all | solution.py:115
  127.8 2.9 %fusion.45 = bf16[1,8,32,128]{3,1,2,0:T(8,128)(2,1)S(1)} fusion(bf16[32,512,128]{2,1,0:T(8,128)(2,1)} %param.35, bf16[8,32,512]{2,1,0:T(8,128)(2,1)S(1)} %bitcast.180), kind=kOutput, calls=%fused_computation.69 | convolution fusion | flops 33587200 | bytes 4521984 | tf_op jit(solution)/shard_map/rhl,hld->rhd/dot_general | solution.py:121
  130.8 1.5 broadcast_select_fusion.2
  132.6 1.9 %while.95 = (s32[]{:T(128)}, f32[2,128,1024]{1,2,0:T(8,128)S(1)}, s32[]{:T(128)}, s32[2]{0:T(128)S(1)}, bf16[2,1024,576]{1,2,0:T(8,128)(2,1)S(1)}, /*index=5*/bf...) while((s32[]{:T(128)}, f32[2,128,1024]{1,2,0:T(8,128)S(1)}, ...), condition=%wide.region_18.19_spmd.clone, body=%wide.region_17.18_spmd.clone.sunk | while | flops 151258624 | bytes 2007207 | solution.py:40
  132.7 1.6 fusion.146
  136.7 2.1 %while.96 = (s32[]{:T(128)}, f32[2,128,1024]{1,2,0:T(8,128)S(1)}, s32[]{:T(128)}, s32[2]{0:T(128)S(1)}, bf16[2,1024,576]{1,2,0:T(8,128)(2,1)}, /*index=5*/bf16[2...) while((s32[]{:T(128)}, f32[2,128,1024]{1,2,0:T(8,128)S(1)}, s32[]{:T(128)}, ...), condition=%wide.region_26.27_spmd.clone, body=%wide.region_25.26_spmd.clone.sunk | while | flops 151258624 | bytes 2007207 | solution.py:40
  136.8 2.0 %fusion.149 = f32[2,128,1024]{1,2,0:T(8,128)S(1)} fusion(f32[2,128,1024]{1,2,0:T(8,128)S(1)} %get-tuple-element.929, s32[]{:T(128)S(6)} %select_n.192, bf16[2,128,576]{1,2,0:T(8,128)(2,1)} %get-tuple-element.943, bf16[2,1024,576]{1,2,0:T(8,128)(2,1)} %get-tuple-element.942, pred[2,512]{1,0:T(4,128)(4,1)S(1)} %broadcast_compare_fusion.11), kind=kOutput, calls=%fused_computation.47.clone.1 | convolution fusion | flops 151257088 | bytes 2001920 | tf_op jit(solution)/shard_map/while/body/rhc,rtc->rht/dot_general | solution.py:32
  141.5 3.1 %copy.99 = bf16[2,1024,576]{2,1,0:T(8,128)(2,1)S(1)} copy(bf16[2,1024,576]{1,2,0:T(8,128)(2,1)} %get-tuple-element.1151) | data formatting | bytes 4718592 | tf_op jit(solution)/shard_map/while | solution.py:67
  144.6 2.3 %while.92 = (s32[]{:T(128)}, f32[2,128,512]{2,1,0:T(8,128)}, s32[]{:T(128)}, bf16[2,128,1024]{1,2,0:T(8,128)(2,1)}, bf16[2,1024,576]{2,1,0:T(8,128)(2,1)S(1)}, /*index=5*/s32[]{:T(128)}, s32[]{:T(128)}, s32[]{:T(128)}, s32[]{:T(128)}) while((s32[]{:T(128)}, f32[2,128,512]{2,1,0:T(8,128)}, s32[]{:T(128)}, bf16[2,128,1024]{1,2,0:T(8,128)(2,1)}, ...), condition=%wide.region_32.33_spmd, body=%wide.region_31.32_spmd.sunk | while | flops 134348800 | bytes 2360467 | solution.py:67
  144.6 2.3 %convolution_add_fusion.11 = f32[2,128,512]{2,1,0:T(8,128)} fusion(f32[2,128,512]{2,1,0:T(8,128)} %get-tuple-element.958, bf16[2,1024,576]{2,1,0:T(8,128)(2,1)S(1)} %get-tuple-element.970, s32[]{:T(128)S(6)} %select_n.184, bf16[2,128,1024]{1,2,0:T(8,128)(2,1)} %get-tuple-element.969), kind=kOutput, calls=%fused_computation.16.clone.1 | convolution fusion | flops 134348800 | bytes 2360320 | tf_op jit(solution)/shard_map/while/body/rht,rtl->rhl/dot_general | solution.py:63
  149.8 15.5 %all-to-all-start.7 = ((bf16[4,2,32,512]{3,2,1,0:T(8,128)(2,1)}), bf16[4,2,32,512]{3,2,1,0:T(8,128)(2,1)S(1)}, u32[]{:S(2)}, u32[]{:S(2)}) async-start(bf16[4,2,32,512]{3,2,1,0:T(8,128)(2,1)} %pad_maximum_fusion.8), calls=%async_computation.7 | async-start | bytes 524288 | tf_op jit(solution)/shard_map/all_to_all | solution.py:115
  167.5 6.5 %all-to-all-done.7 = bf16[4,2,32,512]{3,2,1,0:T(8,128)(2,1)S(1)} async-done(((bf16[4,2,32,512]{3,2,1,0:T(8,128)(2,1)}), bf16[4,2,32,512]{3,2,1,0:T(8,128)(2,1)S(1)}, u32[]{:S(2)}, u32[]{:S(2)}) %all-to-all-start.7) | async-done | bytes 262176 | tf_op jit(solution)/shard_map/all_to_all | solution.py:115
  174.0 4.1 %all-to-all-start.5 = ((bf16[4,2,32,512]{3,2,1,0:T(8,128)(2,1)}), bf16[4,2,32,512]{3,2,1,0:T(8,128)(2,1)S(1)}, u32[]{:S(2)}, u32[]{:S(2)}) async-start(bf16[4,2,32,512]{3,2,1,0:T(8,128)(2,1)} %pad_maximum_fusion.7), calls=%async_computation.5 | async-start | bytes 524288 | tf_op jit(solution)/shard_map/all_to_all | solution.py:115
  178.1 3.1 %fusion.44 = bf16[1,8,32,128]{3,1,2,0:T(8,128)(2,1)S(1)} fusion(bf16[32,512,128]{2,1,0:T(8,128)(2,1)} %param.35, bf16[8,32,512]{2,1,0:T(8,128)(2,1)} %bitcast.12), kind=kOutput, calls=%fused_computation.68 | convolution fusion | flops 33587200 | bytes 4521984 | tf_op jit(solution)/shard_map/rhl,hld->rhd/dot_general | solution.py:121
  182.3 2.5 %all-to-all-done.5 = bf16[4,2,32,512]{3,2,1,0:T(8,128)(2,1)S(1)} async-done(((bf16[4,2,32,512]{3,2,1,0:T(8,128)(2,1)}), bf16[4,2,32,512]{3,2,1,0:T(8,128)(2,1)S(1)}, u32[]{:S(2)}, u32[]{:S(2)}) %all-to-all-start.5) | async-done | bytes 262176 | tf_op jit(solution)/shard_map/all_to_all | solution.py:115
  184.8 2.9 %fusion.46 = bf16[1,8,32,128]{3,1,2,0:T(8,128)(2,1)S(1)} fusion(bf16[32,512,128]{2,1,0:T(8,128)(2,1)} %param.35, bf16[8,32,512]{2,1,0:T(8,128)(2,1)S(1)} %bitcast.181), kind=kOutput, calls=%fused_computation.70 | convolution fusion | flops 33587200 | bytes 4521984 | tf_op jit(solution)/shard_map/rhl,hld->rhd/dot_general | solution.py:121
  (135 shorter events, 41.5 us)
Async XLA Ops:
  0.0 6.4 %copy-start.9 = (bf16[4,8,32,64]{3,2,1,0:T(8,128)(2,1)S(1)}, bf16[4,8,32,64]{3,2,1,0:T(8,128)(2,1)}, u32[]{:S(2)}) copy-start(bf16[4,8,32,64]{3,2,1,0:T(8,128)(2,1)} %param.33) | copy-start | bytes 393220
  0.0 6.5 %copy-start.10 = (bf16[4,8,32,128]{3,2,1,0:T(8,128)(2,1)S(1)}, bf16[4,8,32,128]{3,2,1,0:T(8,128)(2,1)}, u32[]{:S(2)}) copy-start(bf16[4,8,32,128]{3,2,1,0:T(8,128)(2,1)} %param.32) | copy-start | bytes 786436
  0.9 21.2 %collective-permute-start = (bf16[1,4,576]{2,1,0:T(4,128)(2,1)S(1)}, bf16[1,4,576]{2,1,0:T(4,128)(2,1)S(1)}, u32[]{:S(2)}, u32[]{:S(2)}) collective-permute-start(bf16[1,4,576]{2,1,0:T(4,128)(2,1)S(1)} %slice.181), channel_id=1, source_target_pairs={{0,4},{4,8},{8,12},{12,16},{16,20},{20,24},{24,28},{28,0},{1,5},{5... | collective-permute-start | bytes 13832 | tf_op jit(solution)/shard_map/ppermute | solution.py:17
  3.8 73.6 %collective-permute-start.3 = (bf16[1,1024,576]{1,2,0:T(8,128)(2,1)}, bf16[1,1024,576]{1,2,0:T(8,128)(2,1)}, u32[]{:S(2)}, u32[]{:S(2)}) collective-permute-start(bf16[1,1024,576]{1,2,0:T(8,128)(2,1)} %slice.168), channel_id=1, source_target_pairs={{0,4},{4,8},{8,12},{12,16},{16,20},{20,24},{24,28},{28,0},{1,5},{5... | collective-permute-start | bytes 3538952 | tf_op jit(solution)/shard_map/ppermute | solution.py:17
  10.2 28.7 %all-to-all-start.2 = ((bf16[8,32,576]{2,1,0:T(8,128)(2,1)}), bf16[8,32,576]{2,1,0:T(8,128)(2,1)S(1)}, u32[]{:S(2)}, u32[]{:S(2)}) async-start(bf16[8,32,576]{2,1,0:T(8,128)(2,1)} %copy.83), calls=%async_computation.2 | async-start | bytes 655360 | tf_op jit(solution)/shard_map/all_to_all | solution.py:110
  15.1 3.4 %copy-start = (bf16[32,128,512]{2,1,0:T(8,128)(2,1)S(1)}, bf16[32,128,512]{2,1,0:T(8,128)(2,1)}, u32[]{:S(2)}) copy-start(bf16[32,128,512]{2,1,0:T(8,128)(2,1)} %param.34) | copy-start | bytes 12582916
  19.2 4.5 %copy-start.11 = (s32[64]{0:T(128)S(1)}, s32[64]{0:T(128)}, u32[]{:S(2)}) copy-start(s32[64]{0:T(128)} %param.38) | copy-start | bytes 772
  22.1 4.6 %collective-permute-start.1 = (bf16[1,4,576]{2,1,0:T(4,128)(2,1)S(1)}, bf16[1,4,576]{2,1,0:T(4,128)(2,1)S(1)}, u32[]{:S(2)}, u32[]{:S(2)}) collective-permute-start(bf16[1,4,576]{2,1,0:T(4,128)(2,1)S(1)} %get-tuple-element.624), channel_id=1, source_target_pairs={{0,8},{4,12},{8,16},{12,20},{16,24},{20,28},{24,0},{28,4},{1,9},{5... | collective-permute-start | bytes 13832 | tf_op jit(solution)/shard_map/ppermute | solution.py:17
  26.7 12.1 %collective-permute-start.2 = (bf16[1,4,576]{2,1,0:T(4,128)(2,1)S(1)}, bf16[1,4,576]{2,1,0:T(4,128)(2,1)S(1)}, u32[]{:S(2)}, u32[]{:S(2)}) collective-permute-start(bf16[1,4,576]{2,1,0:T(4,128)(2,1)S(1)} %broadcast_select_fusion.4), channel_id=1, source_target_pairs={{0,16},{4,20},{8,24},{12,28},{16,0},{20,4},{24,8},{28,12},{1,17},{... | collective-permute-start | bytes 13832 | tf_op jit(solution)/shard_map/ppermute | solution.py:17
  38.9 17.1 %all-to-all-start = ((bf16[8,32,576]{2,1,0:T(8,128)(2,1)}), bf16[8,32,576]{2,1,0:T(8,128)(2,1)S(1)}, u32[]{:S(2)}, u32[]{:S(2)}) async-start(bf16[8,32,576]{2,1,0:T(8,128)(2,1)} %copy.73), calls=%async_computation | async-start | bytes 655360 | tf_op jit(solution)/shard_map/all_to_all | solution.py:110
  56.1 0.7 copy-start.8
  56.8 30.9 %all-to-all-start.4 = ((bf16[8,32,576]{2,1,0:T(8,128)(2,1)}), bf16[8,32,576]{2,1,0:T(8,128)(2,1)S(1)}, u32[]{:S(2)}, u32[]{:S(2)}) async-start(bf16[8,32,576]{2,1,0:T(8,128)(2,1)} %copy.93), calls=%async_computation.4 | async-start | bytes 655360 | tf_op jit(solution)/shard_map/all_to_all | solution.py:110
  81.0 24.6 %collective-permute-start.4 = (bf16[1,1024,576]{1,2,0:T(8,128)(2,1)}, bf16[1,1024,576]{1,2,0:T(8,128)(2,1)}, u32[]{:S(2)}, u32[]{:S(2)}) collective-permute-start(bf16[1,1024,576]{1,2,0:T(8,128)(2,1)} %get-tuple-element.594), channel_id=1, source_target_pairs={{0,8},{4,12},{8,16},{12,20},{16,24},{20,28},{24,0},{28,4},{1,9},{5... | collective-permute-start | bytes 3538952 | tf_op jit(solution)/shard_map/ppermute | solution.py:17
  87.7 21.5 %all-to-all-start.6 = ((bf16[8,32,576]{2,1,0:T(8,128)(2,1)}), bf16[8,32,576]{2,1,0:T(8,128)(2,1)S(1)}, u32[]{:S(2)}, u32[]{:S(2)}) async-start(bf16[8,32,576]{2,1,0:T(8,128)(2,1)} %copy.103), calls=%async_computation.6 | async-start | bytes 655360 | tf_op jit(solution)/shard_map/all_to_all | solution.py:110
  107.0 23.8 %collective-permute-start.5 = (bf16[1,1024,576]{1,2,0:T(8,128)(2,1)S(1)}, bf16[1,1024,576]{1,2,0:T(8,128)(2,1)}, u32[]{:S(2)}, u32[]{:S(2)}) collective-permute-start(bf16[1,1024,576]{1,2,0:T(8,128)(2,1)S(1)} %broadcast_select_fusion.1), channel_id=1, source_target_pairs={{0,16},{4,20},{8,24},{12,28},{16,0},{20,4},{24,8},{28,12},{1,17},{... | collective-permute-start | bytes 3538952 | tf_op jit(solution)/shard_map/ppermute | solution.py:17
  109.2 14.5 %all-to-all-start.3 = ((bf16[4,2,32,512]{3,2,1,0:T(8,128)(2,1)}), bf16[4,2,32,512]{3,2,1,0:T(8,128)(2,1)S(1)}, u32[]{:S(2)}, u32[]{:S(2)}) async-start(bf16[4,2,32,512]{3,2,1,0:T(8,128)(2,1)} %pad_maximum_fusion.6), calls=%async_computation.3 | async-start | bytes 524288 | tf_op jit(solution)/shard_map/all_to_all | solution.py:115
  117.9 12.7 %copy-start.6 = (bf16[4,2,32,576]{3,2,0,1:T(8,128)(2,1)}, bf16[4,2,32,576]{3,2,0,1:T(8,128)(2,1)S(1)}, u32[]{:S(2)}) copy-start(bf16[4,2,32,576]{3,2,0,1:T(8,128)(2,1)S(1)} %copy.104) | copy-start | bytes 884740
  123.7 26.1 %all-to-all-start.1 = ((bf16[4,2,32,512]{3,2,1,0:T(8,128)(2,1)}), bf16[4,2,32,512]{3,2,1,0:T(8,128)(2,1)}, u32[]{:S(2)}, u32[]{:S(2)}) async-start(bf16[4,2,32,512]{3,2,1,0:T(8,128)(2,1)} %pad_maximum_fusion.5), calls=%async_computation.1 | async-start | bytes 524288 | tf_op jit(solution)/shard_map/all_to_all | solution.py:115
  130.7 1.6 copy-start.5
  134.6 1.0 copy-start.2
  134.6 1.7 copy-start.4
  136.7 2.2 %copy-start.7 = (bf16[4,2,32,576]{3,2,0,1:T(8,128)(2,1)S(1)}, bf16[4,2,32,576]{3,2,0,1:T(8,128)(2,1)}, u32[]{:S(2)}) copy-start(bf16[4,2,32,576]{3,2,0,1:T(8,128)(2,1)} %copy-done.6) | copy-start | bytes 884740
  146.9 1.9 %copy-start.3 = (f32[2,128,1024]{1,2,0:T(8,128)S(1)}, f32[2,128,1024]{1,2,0:T(8,128)}, u32[]{:S(2)}) copy-start(f32[2,128,1024]{1,2,0:T(8,128)} %copy-done.2) | copy-start | bytes 3145732
  149.8 24.1 %all-to-all-start.7 = ((bf16[4,2,32,512]{3,2,1,0:T(8,128)(2,1)}), bf16[4,2,32,512]{3,2,1,0:T(8,128)(2,1)S(1)}, u32[]{:S(2)}, u32[]{:S(2)}) async-start(bf16[4,2,32,512]{3,2,1,0:T(8,128)(2,1)} %pad_maximum_fusion.8), calls=%async_computation.7 | async-start | bytes 524288 | tf_op jit(solution)/shard_map/all_to_all | solution.py:115
  174.0 10.9 %all-to-all-start.5 = ((bf16[4,2,32,512]{3,2,1,0:T(8,128)(2,1)}), bf16[4,2,32,512]{3,2,1,0:T(8,128)(2,1)S(1)}, u32[]{:S(2)}, u32[]{:S(2)}) async-start(bf16[4,2,32,512]{3,2,1,0:T(8,128)(2,1)} %pad_maximum_fusion.7), calls=%async_computation.5 | async-start | bytes 524288 | tf_op jit(solution)/shard_map/all_to_all | solution.py:115
  178.1 3.5 %copy-start.1 = (bf16[32,512,128]{2,1,0:T(8,128)(2,1)S(1)}, bf16[32,512,128]{2,1,0:T(8,128)(2,1)}, u32[]{:S(2)}) copy-start(bf16[32,512,128]{2,1,0:T(8,128)(2,1)} %param.35) | copy-start | bytes 12582916
